TPU v7x, 32 devices: a whole 2x2x4 slice. The times are simulated.
32 devices in a mesh: rep: 8 (over y, x, core), fsdp: 4 (over z).
Axes of the slice: x: 2, y: 2, z: 4, core: 2. Of those that a mesh axis runs over, the one named last changes fastest.
Arguments:
- tokens: bfloat16 [4096, 4096], P('rep', 'fsdp'), may hold values from -6 to 6
- gate_weight: bfloat16 [4096, 7168], P('rep', 'fsdp'), may hold values from -0.09375 to 0.09375
- up_act: bfloat16 [4096, 7168], P('rep', 'fsdp'), may hold values from -6 to 6
- cotangent: bfloat16 [4096, 7168], P('rep', 'fsdp'), may hold values from -0.099609375 to 0.099609375
Outputs:
- grad_sum: bfloat16 [4096, 7168], P('rep', 'fsdp')
- curvature: float32 [7168], P('fsdp')
- spread: float32 [7168], P('fsdp')
All inputs are finite; a program needn't handle non-finite values.
Results may differ from a plain program's by a relative error of at most 0.024.
Values may be sent and summed in bfloat16 or wider, within the bound.
A program may use at most 128 MiB of HBM per device.

v0:
```python
import jax
import jax.numpy as jnp
from jax import lax
from jax.sharding import PartitionSpec as P


def shards(tokens, gate_weight, up_act, cotangent):
    features_all = lax.all_gather(tokens, "fsdp", axis=1, tiled=True)
    replicas = lax.axis_size("rep")

    def add_rows(block_rows):
        return jnp.dot(features_all, block_rows, preferred_element_type=jnp.float32)

    gate_pre = add_rows(lax.all_gather(gate_weight, "rep", axis=0, tiled=True))
    sigmoid_gate = jax.nn.sigmoid(gate_pre)
    deriv_one = sigmoid_gate * (1.0 + gate_pre * (1.0 - sigmoid_gate))
    deriv_two = sigmoid_gate * (1.0 - sigmoid_gate) * (2.0 + gate_pre * (1.0 - 2.0 * sigmoid_gate))
    weighted = cotangent.astype(jnp.float32) * up_act.astype(jnp.float32)
    token_coeff = (weighted * deriv_one).astype(jnp.bfloat16)
    bend_weight = weighted * deriv_two
    rep_grad = lax.dot_general(
        features_all, token_coeff, (((0,), (0,)), ((), ())), preferred_element_type=jnp.float32
    ).astype(jnp.bfloat16)
    own_proj = jnp.dot(features_all, rep_grad, preferred_element_type=jnp.float32)
    grad_shard = lax.psum_scatter(
        rep_grad.astype(jnp.float32).astype(jnp.bfloat16), "rep", scatter_dimension=0, tiled=True
    )
    mean_proj = add_rows(lax.all_gather(grad_shard, "rep", axis=0, tiled=True)) / replicas
    deviate = own_proj - mean_proj
    curv_part = jnp.sum(bend_weight * mean_proj * mean_proj, axis=0)
    spread_part = jnp.sum(bend_weight * deviate * deviate, axis=0)
    curvature, spread_total = lax.psum((curv_part, spread_part), "rep")
    return (grad_shard, curvature, spread_total / (replicas - 1))


def solution(mesh):
    placed = (P("rep", "fsdp"), P("rep", "fsdp"), P("rep", "fsdp"), P("rep", "fsdp"))
    return jax.shard_map(
        shards,
        mesh=mesh,
        in_specs=placed,
        out_specs=(P("rep", "fsdp"), P("fsdp"), P("fsdp")),
        check_vma=False,
    )
```

profile of v0, /device:TPU:0, one launch (start us, length us, event | category | flops | bytes accessed | tf_op | source)
XLA Modules:
  0.0 455.3 jit_solution(8435540799089013819)
XLA Ops:
  7.2 0.0 all-gather.4.cloned.1.call-start
  7.2 0.7 all-gather.4.cloned.1.call-update
  7.9 0.0 all-gather.6.cloned.1.call-start
  7.9 0.7 all-gather.6.cloned.1.call-update
  8.6 0.0 copy-start.2
  8.7 0.0 reduce-scatter.2.cloned.1.call-start
  8.7 84.3 %all-gather.4.cloned.1.call-done = bf16[512,4096]{1,0:T(8,128)(2,1)} async-done(((bf16[512,1024]{1,0:T(8,128)(2,1)}), bf16[512,4096]{1,0:T(8,128)(2,1)}) %all-gather.4.cloned.1.call-update) | async-done | bytes 4194320 | tf_op jit(solution)/shard_map/all_gather | solution.py:8
  93.0 81.3 %all-gather.6.cloned.1.call-done = bf16[4096,1792]{1,0:T(8,128)(2,1)} async-done(((bf16[512,1792]{1,0:T(8,128)(2,1)}), bf16[4096,1792]{1,0:T(8,128)(2,1)}) %all-gather.6.cloned.1.call-update) | async-done | bytes 14680080 | tf_op jit(solution)/shard_map/all_gather | solution.py:14
  174.3 0.0 copy-start
  174.3 0.0 copy-start.3
  174.3 16.7 %fusion.11 = f32[512,1792]{1,0:T(8,128)} fusion(bf16[512,4096]{1,0:T(8,128)(2,1)} %all-gather.4.cloned.1.call-done, bf16[4096,1792]{1,0:T(8,128)(2,1)} %all-gather.6.cloned.1.call-done), kind=kOutput, calls=%fused_computation.20 | convolution fusion | flops 7516192768 | bytes 22544384 | tf_op jit(solution)/shard_map/dot_general | solution.py:12
  191.0 0.0 copy-done.2
  191.0 0.0 copy-done
  191.0 0.0 copy-done.3
  191.0 15.3 %convolution_convert_fusion = bf16[1792,4096]{1,0:T(8,128)(2,1)} fusion(bf16[512,4096]{1,0:T(8,128)(2,1)S(1)} %copy-done, f32[512,1792]{1,0:T(8,128)} %fusion.11, bf16[512,1792]{1,0:T(8,128)(2,1)S(1)} %copy-done.2, bf16[512,1792]{1,0:T(8,128)(2,1)S(1)} %copy-done.3), kind=kOutput, calls=%fused_computation | convolution fusion | flops 7534542848 | bytes 26214400 | tf_op jit(solution)/shard_map/dot_general | solution.py:21
  206.3 0.0 reduce-scatter.2.cloned.1.call-update
  206.4 0.2 all-gather.8.cloned.1.call-start
  206.6 102.2 %reduce-scatter.2.cloned.1.call-done = bf16[512,1792]{0,1:T(8,128)(2,1)} async-done(((bf16[4096,1792]{0,1:T(8,128)(2,1)}), bf16[512,1792]{0,1:T(8,128)(2,1)}) %reduce-scatter.2.cloned.1.call-update) | async-done | bytes 1835024 | tf_op jit(solution)/shard_map/reduce_scatter | solution.py:25
  308.8 0.0 all-gather.8.cloned.1.call-update
  308.8 3.8 copy.7
  312.6 81.6 %all-gather.8.cloned.1.call-done = bf16[4096,1792]{0,1:T(8,128)(2,1)} async-done(((bf16[512,1792]{0,1:T(8,128)(2,1)}), bf16[4096,1792]{0,1:T(8,128)(2,1)}) %all-gather.8.cloned.1.call-update) | async-done | bytes 14680080 | tf_op jit(solution)/shard_map/all_gather | solution.py:28
  394.2 0.0 copy-start.1
  394.2 0.0 copy-start.4
  394.2 0.0 copy-start.5
  394.2 16.5 %fusion.6 = (f32[1792]{0:T(1024)S(1)}, f32[1792,512]{0,1:T(8,128)S(1)}) fusion(f32[512,1792]{1,0:T(8,128)} %fusion.11, bf16[512,1792]{1,0:T(8,128)(2,1)S(1)} %copy-done.2, bf16[512,1792]{1,0:T(8,128)(2,1)} %param.7, bf16[4096,1792]{0,1:T(8,128)(2,1)} %all-gather.8.cloned.1.call-done, bf16[512,4096]{1,0:T(8,128)(2,1)} %all-gather.4.cloned.1.call-done), kind=kOutput, calls=%fused_computation.11 | convolution fusion | flops 7532705792 | bytes 29891584 | tf_op jit(solution)/shard_map/dot_general | solution.py:12
  410.8 0.0 copy-done.1
  410.8 0.0 copy-done.4
  410.8 0.0 copy-done.5
  410.8 13.8 %fusion.7 = f32[1792]{0:T(1024)S(1)} fusion(f32[1792,512]{0,1:T(8,128)S(1)} %get-tuple-element.9, bf16[1792,4096]{1,0:T(8,128)(2,1)} %convolution_convert_fusion, bf16[512,4096]{1,0:T(8,128)(2,1)S(1)} %copy-done.1, f32[512,1792]{1,0:T(8,128)S(1)} %copy-done.5, bf16[512,1792]{1,0:T(8,128)(2,1)S(1)} %copy-done.2, bf16[512,1792]{1,0:T(8,128)(2,1)S(1)} %copy-done.4), kind=kOutput, calls=%fused_computation.12 | convolution fusion | flops 7532705792 | bytes 29891584 | tf_op jit(solution)/shard_map/dot_general | solution.py:24
  424.7 23.5 %all-reduce = (f32[1792]{0:T(1024)}, f32[1792]{0:T(1024)S(1)}) all-reduce(f32[1792]{0:T(1024)S(1)} %get-tuple-element.8, f32[1792]{0:T(1024)S(1)} %fusion.7), channel_id=1, replica_groups=mesh['rep'=8,'fsdp'=4] {'rep'}, use_global_device_ids=true, to_apply=%region_2.0 | all-reduce | flops 3584 | bytes 28672 | tf_op jit(solution)/shard_map/psum | solution.py:32
  448.1 0.6 broadcast_multiply_fusion
Async XLA Ops:
  7.2 85.9 %all-gather.4.cloned.1.call-start = ((), (), s32[]{:S(2)}) async-start(), calls=%async_computation.1 | async-start | bytes 5242880 | tf_op jit(solution)/shard_map/all_gather | solution.py:8
  7.9 166.4 %all-gather.6.cloned.1.call-start = ((), (), s32[]{:S(2)}) async-start(), calls=%async_computation.2 | async-start | bytes 16515072 | tf_op jit(solution)/shard_map/all_gather | solution.py:14
  8.6 182.4 %copy-start.2 = (bf16[512,1792]{1,0:T(8,128)(2,1)S(1)}, bf16[512,1792]{1,0:T(8,128)(2,1)}, u32[]{:S(2)}) copy-start(bf16[512,1792]{1,0:T(8,128)(2,1)} %param.6) | copy-start | bytes 5505028
  8.7 300.1 %reduce-scatter.2.cloned.1.call-start = ((), (), s32[]{:S(2)}) async-start(), calls=%async_computation.3 | async-start | bytes 16515072 | tf_op jit(solution)/shard_map/reduce_scatter | solution.py:25
  174.3 16.7 %copy-start = (bf16[512,4096]{1,0:T(8,128)(2,1)S(1)}, bf16[512,4096]{1,0:T(8,128)(2,1)}, u32[]{:S(2)}) copy-start(bf16[512,4096]{1,0:T(8,128)(2,1)} %all-gather.4.cloned.1.call-done) | copy-start | bytes 12582916
  174.3 16.7 %copy-start.3 = (bf16[512,1792]{1,0:T(8,128)(2,1)S(1)}, bf16[512,1792]{1,0:T(8,128)(2,1)}, u32[]{:S(2)}) copy-start(bf16[512,1792]{1,0:T(8,128)(2,1)} %param.7) | copy-start | bytes 5505028
  206.4 187.9 %all-gather.8.cloned.1.call-start = ((), (), s32[]{:S(2)}) async-start(), calls=%async_computation.4 | async-start | bytes 16515072 | tf_op jit(solution)/shard_map/all_gather | solution.py:28
  394.2 16.5 %copy-start.1 = (bf16[512,4096]{1,0:T(8,128)(2,1)S(1)}, bf16[512,4096]{1,0:T(8,128)(2,1)}, u32[]{:S(2)}) copy-start(bf16[512,4096]{1,0:T(8,128)(2,1)} %all-gather.4.cloned.1.call-done) | copy-start | bytes 12582916
  394.2 16.6 %copy-start.4 = (bf16[512,1792]{1,0:T(8,128)(2,1)S(1)}, bf16[512,1792]{1,0:T(8,128)(2,1)}, u32[]{:S(2)}) copy-start(bf16[512,1792]{1,0:T(8,128)(2,1)} %param.7) | copy-start | bytes 5505028
  394.2 16.6 %copy-start.5 = (f32[512,1792]{1,0:T(8,128)S(1)}, f32[512,1792]{1,0:T(8,128)}, u32[]{:S(2)}) copy-start(f32[512,1792]{1,0:T(8,128)} %fusion.11) | copy-start | bytes 11010052
Sparse Core Ops, SparseCore 0:
  9.5 83.4 all-gather.3
  94.9 79.3 all-gather.5
  206.5 102.2 reduce-scatter.1
  310.5 83.7 all-gather.7
where the time goes:
time: 456 us; the launch traced here: 455 us
  waiting for transfers between devices  351 us (77%)
  matrix products  62.4 us (14%)
  blocking collectives  23.5 us (5%)
  between operations  13.8 us (3%)
    reduce_scatter x1, waiting for transfers between devices, shards(): lax.psum_scatter(rep_grad.astype(jnp.float32).astype(jnp.bfloat16), 'rep'...  102 us
    all_gather x1, waiting for transfers between devices, shards(): features_all = lax.all_gather(tokens, 'fsdp', axis=1, tiled=True)  84.3 us
    all_gather x1, waiting for transfers between devices, shards(): lax.all_gather(grad_shard, 'rep', axis=0, tiled=True)  81.6 us
    all_gather x1, waiting for transfers between devices, shards(): gate_pre = add_rows(lax.all_gather(gate_weight, 'rep', axis=0, tiled=True))  81.3 us
    dot_general x2, matrix products, add_rows(): return jnp.dot(features_all, block_rows, preferred_element_type=jnp.float32)  33.2 us
    psum x1, blocking collectives, shards(): curvature, spread_total = lax.psum((curv_part, spread_part), 'rep')  23.5 us
    dot_general x1, matrix products, shards(): lax.dot_general(features_all, token_coeff, (((0,), (0,)), ((), ())), pref...  15.3 us
    dot_general x1, matrix products, shards(): jnp.dot(features_all, rep_grad, preferred_element_type=jnp.float32)  13.8 us
  transfers between devices with their start and end apart: 4, of which 4 were waited for; matrix products, arithmetic and copies ran while one was open for 1% of the time, Pallas kernels for 0%

commit v1 on v0

v1 whole, which is shorter than its diff:
```python
import functools

import jax
import jax.numpy as jnp
from jax import lax
from jax.experimental import pallas as pl
from jax.experimental.pallas import tpu as pltpu
from jax.sharding import PartitionSpec as P

MESH = pl.DeviceIdType.MESH
ANY = pl.BlockSpec(memory_space=pl.ANY)


def rep_bits(r):
    return r // 4, (r // 2) % 2, r % 2


def flip(r, m):
    y, x, c = rep_bits(r)
    y = 1 - y if m & 4 else y
    x = 1 - x if m & 2 else x
    c = 1 - c if m & 1 else c
    return y * 4 + x * 2 + c


def when(cond, fn):
    if cond is True:
        fn()
    else:
        pl.when(cond)(fn)


def both(a, b):
    if a is True:
        return b
    if b is True:
        return a
    return jnp.logical_and(a, b)


def greet(zs, r, z, masks, reach):
    barrier = pltpu.get_barrier_semaphore()
    for m in masks:
        pl.semaphore_signal(barrier, inc=1, device_id=(flip(r, m), z), device_id_type=MESH)
    if not reach:
        pl.semaphore_wait(barrier, len(masks))
        return

    @pl.when(z > 0)
    def _():
        pl.semaphore_signal(barrier, inc=1, device_id=(r, z - 1), device_id_type=MESH)

    @pl.when(z < zs - 1)
    def _():
        pl.semaphore_signal(barrier, inc=1, device_id=(r, z + 1), device_id_type=MESH)

    edge = jnp.where(z > 0, 1, 0) + jnp.where(z < zs - 1, 1, 0)
    pl.semaphore_wait(barrier, len(masks) + edge)


def gather_kernel(zs, nr, t_ref, w_ref, u_ref, ta, wa, ua, tv, wv, uv, s_x, s_y, s_u, s_d, s_c, r_t, r_c, s_a, r_a, s_l):
    r, z = lax.axis_index("rep"), lax.axis_index("fsdp")
    rows, feats = t_ref.shape
    part = rows // 4
    greet(zs, r, z, range(1, nr), True)
    pending = []

    def region(ref, m, q, zo):
        return ref.at[
            pl.ds(pl.multiple_of(flip(r, m) * rows + q * part, part), part),
            pl.ds(pl.multiple_of(zo * feats, feats), feats),
        ]

    def rsem(m, q, zo):
        return ((m // 2) * 4 + q) * zs + zo

    def push(cond, m, q, zo, way, slot):
        own = m == 0 and zo is z
        src = t_ref.at[pl.ds(q * part, part), :] if own else region(ta, m, q, zo)
        dst = region(ta, m, q, zo)
        if way == "x":
            to, sem, kind, rs = (flip(r, 2), z), s_x, m ^ 2, r_t
        elif way == "y":
            to, sem, kind, rs = (flip(r, 4), z), s_y, m ^ 4, r_t
        elif way == "u":
            to, sem, kind, rs = (r, z + 1), s_u, m, r_t
        elif way == "d":
            to, sem, kind, rs = (r, z - 1), s_d, m, r_t
        else:
            to, sem, kind, rs = (flip(r, 1), z), s_c, m, r_c
        copy = pltpu.make_async_remote_copy(
            src_ref=src, dst_ref=dst, send_sem=sem.at[slot], recv_sem=rs.at[rsem(kind, q, zo)],
            device_id=to, device_id_type=MESH,
        )
        when(cond, copy.start)
        pending.append((cond, copy))

    def xy_slot(q, zo, relay):
        base = 3 if q >= 2 else 0
        return base + (zo * 3 if q >= 2 else 0) + (2 if relay else q % 2)

    def z_slot(m, q, zo):
        return (((m // 2) * 2 + q) if q < 2 else 8 + q - 2) * zs + zo

    def go_up(cond, m, q, zo):
        push(both(cond, z < zs - 1), m, q, zo, "u", z_slot(m, q, zo))

    def go_down(cond, m, q, zo):
        push(both(cond, z > 0), m, q, zo, "d", z_slot(m, q, zo))

    def go_xy(cond, q, zo):
        push(cond, 0, q, zo, "x", xy_slot(q, zo, False))
        push(cond, 0, q, zo, "y", xy_slot(q, zo, False))

    def go_core(cond, m, q, zo):
        push(cond, m, q, zo, "c", rsem(m, q, zo))

    keep = pltpu.make_async_copy(t_ref, tv, s_l.at[0])
    keep_w = pltpu.make_async_copy(w_ref.at[r], wv, s_l.at[1])
    keep_u = pltpu.make_async_copy(u_ref.at[r], uv, s_l.at[2])
    for copy in (keep, keep_w, keep_u):
        copy.start()
    for q in (0, 1):
        go_xy(True, q, z)
    for q in (2, 3, 0, 1):
        go_up(True, 0, q, z)
        go_down(True, 0, q, z)
    swaps = []
    for a, (src, dst) in enumerate(((w_ref, wa), (u_ref, ua))):
        for m in range(1, nr):
            copy = pltpu.make_async_remote_copy(
                src_ref=src.at[flip(r, m)], dst_ref=dst.at[r],
                send_sem=s_a.at[a, m], recv_sem=r_a.at[a, m],
                device_id=(flip(r, m), z), device_id_type=MESH,
            )
            swaps.append(copy)
    for copy in swaps[: nr - 1]:
        copy.start()
    for q in (2, 3):
        go_xy(True, q, z)
    for copy in swaps[nr - 1 :]:
        copy.start()
    for q in range(4):
        go_core(True, 0, q, z)
    for copy in (keep, keep_w, keep_u):
        copy.wait()
    mine = ta.at[
        pl.ds(pl.multiple_of(r * rows, rows), rows), pl.ds(pl.multiple_of(z * feats, feats), feats)
    ]
    keep = pltpu.make_async_copy(tv, mine, s_l.at[0])
    keep_w = pltpu.make_async_copy(wv, wa.at[r], s_l.at[1])
    keep_u = pltpu.make_async_copy(uv, ua.at[r], s_l.at[2])
    for copy in (keep, keep_w, keep_u):
        copy.start()

    items = []
    hops = {0: 0, 2: 1, 4: 1, 6: 2}
    for m in (0, 2, 4, 6):
        for d in range(-(zs - 1), zs):
            if m == 0 and d == 0:
                continue
            for q in range(4):
                items.append((hops[m] + abs(d), m if d == 0 or q >= 2 else m, q, d))
    items.sort(key=lambda i: (i[0], abs(i[3])))
    for _, m, q, d in items:
        zo = z if d == 0 else z + d
        valid = True if d == 0 else (zo >= 0 if d < 0 else zo < zs)
        got = pltpu.make_async_copy(region(ta, m, q, zo), region(ta, m, q, zo), r_t.at[rsem(m, q, zo)])
        when(valid, got.wait)
        if q < 2:
            if d == 0:
                if m == 4 and q == 0:
                    push(True, 4, 0, z, "x", xy_slot(0, z, True))
                if m == 2 and q == 1:
                    push(True, 2, 1, z, "y", xy_slot(1, z, True))
                go_up(True, m, q, z)
                go_down(True, m, q, z)
            elif d < 0:
                go_up(valid, m, q, zo)
            else:
                go_down(valid, m, q, zo)
        else:
            if m == 0:
                go_xy(valid, q, zo)
                if d < 0:
                    go_up(valid, 0, q, zo)
                else:
                    go_down(valid, 0, q, zo)
            if m == 4 and q == 2:
                push(valid, 4, 2, zo, "x", xy_slot(2, zo, True))
            if m == 2 and q == 3:
                push(valid, 2, 3, zo, "y", xy_slot(3, zo, True))
        go_core(valid, m, q, zo)
    for copy in (keep, keep_w, keep_u):
        copy.wait()
    for copy in swaps:
        copy.wait()
    for cond, copy in pending:
        when(cond, copy.wait_send)
    for m in (0, 2, 4, 6):
        for q in range(4):
            for zo in range(zs):
                spot = region(ta, m | 1, q, zo)
                pltpu.make_async_copy(spot, spot, r_c.at[rsem(m, q, zo)]).wait()


def gather_all(zs, nr, tokens, w, u):
    rows, feats = tokens.shape
    dma = pltpu.SemaphoreType.DMA
    full = zs * 16
    return pl.pallas_call(
        functools.partial(gather_kernel, zs, nr),
        out_shape=(
            jax.ShapeDtypeStruct((rows * nr, feats * zs), tokens.dtype),
            jax.ShapeDtypeStruct(w.shape, w.dtype),
            jax.ShapeDtypeStruct(u.shape, u.dtype),
        ),
        in_specs=[ANY] * 3,
        out_specs=(ANY,) * 3,
        scratch_shapes=[
            pltpu.VMEM(tokens.shape, tokens.dtype),
            pltpu.VMEM(w.shape[1:], w.dtype),
            pltpu.VMEM(u.shape[1:], u.dtype),
            dma((3 + 3 * zs,)), dma((3 + 3 * zs,)), dma((10 * zs,)), dma((10 * zs,)), dma((full,)),
            dma((full,)), dma((full,)), dma((2, nr)), dma((2, nr)), dma((3,)),
        ],
        compiler_params=pltpu.CompilerParams(collective_id=0, has_side_effects=True),
    )(tokens, w, u)


def return_kernel(nr, g_ref, p_ref, ga, pa, gv, pv, s_a, r_a, s_l):
    r, z = lax.axis_index("rep"), lax.axis_index("fsdp")
    greet(0, r, z, range(1, nr), False)
    swaps = []
    for m in range(1, nr):
        there = flip(r, m)
        for a, (src, dst) in enumerate(((g_ref.at[there], ga.at[r]), (p_ref, pa.at[r]))):
            copy = pltpu.make_async_remote_copy(
                src_ref=src, dst_ref=dst, send_sem=s_a.at[a, m], recv_sem=r_a.at[a, m],
                device_id=(there, z), device_id_type=MESH,
            )
            copy.start()
            swaps.append(copy)
    for src, mid, dst, a in ((g_ref.at[r], gv, ga.at[r], 0), (p_ref, pv, pa.at[r], 1)):
        copy = pltpu.make_async_copy(src, mid, s_l.at[a])
        copy.start()
        copy.wait()
        copy = pltpu.make_async_copy(mid, dst, s_l.at[a])
        copy.start()
        copy.wait()
    for copy in swaps:
        copy.wait()


def give_back(nr, grads, parts):
    dma = pltpu.SemaphoreType.DMA
    return pl.pallas_call(
        functools.partial(return_kernel, nr),
        out_shape=(
            jax.ShapeDtypeStruct(grads.shape, grads.dtype),
            jax.ShapeDtypeStruct((nr,) + parts.shape, parts.dtype),
        ),
        in_specs=[ANY] * 2,
        out_specs=(ANY,) * 2,
        scratch_shapes=[
            pltpu.VMEM(grads.shape[1:], grads.dtype),
            pltpu.VMEM(parts.shape, parts.dtype),
            dma((2, nr)), dma((2, nr)), dma((2,)),
        ],
        compiler_params=pltpu.CompilerParams(collective_id=1, has_side_effects=True),
    )(grads, parts)


def derivatives(gate_pre):
    s = jax.nn.sigmoid(gate_pre)
    one = s * (1.0 + gate_pre * (1.0 - s))
    two = s * (1.0 - s) * (2.0 + gate_pre * (1.0 - 2.0 * s))
    return one, two


def units_split(zs, nr, tokens, gate_weight, up_act, cotangent):
    rows, _ = tokens.shape
    hidden = gate_weight.shape[1]
    cols = hidden // nr

    def by_unit(a):
        return a.reshape(a.shape[0], nr, cols).transpose(1, 0, 2)

    product = cotangent.astype(jnp.float32) * up_act.astype(jnp.float32)
    t_all, w_all, u_all = gather_all(
        zs, nr, tokens, by_unit(gate_weight), by_unit(product.astype(jnp.bfloat16))
    )
    model = t_all.shape[1]
    gate_pre = jnp.dot(t_all, w_all.reshape(model, cols), preferred_element_type=jnp.float32)
    one, two = derivatives(gate_pre)
    weighted = u_all.reshape(nr * rows, cols).astype(jnp.float32)
    coeff = (weighted * one).astype(jnp.bfloat16).reshape(nr, rows, cols)
    bend = weighted * two
    t_rep = t_all.reshape(nr, rows, model)
    rep_grad = lax.dot_general(
        t_rep, coeff, (((1,), (1,)), ((0,), (0,))), preferred_element_type=jnp.float32
    ).astype(jnp.bfloat16)
    own = lax.dot_general(
        t_rep, rep_grad, (((2,), (1,)), ((0,), (0,))), preferred_element_type=jnp.float32
    ).reshape(nr * rows, cols)
    grad_sum = jnp.sum(rep_grad.astype(jnp.float32), axis=0).astype(jnp.bfloat16)
    mean = jnp.dot(t_all, grad_sum, preferred_element_type=jnp.float32) / nr
    dev = own - mean
    curv = jnp.sum(bend * mean * mean, axis=0)
    spread = jnp.sum(bend * dev * dev, axis=0) / (nr - 1)
    parts = jnp.pad(jnp.stack([curv, spread]), ((0, 6), (0, -cols % 128)))
    g_all, p_all = give_back(nr, grad_sum.reshape(nr, model // nr, cols), parts)
    grad_rows = g_all.transpose(1, 0, 2).reshape(model // nr, hidden)
    stats = p_all[:, :, :cols]
    return grad_rows, stats[:, 0].reshape(hidden), stats[:, 1].reshape(hidden)


def tokens_split(tokens, gate_weight, up_act, cotangent):
    features_all = lax.all_gather(tokens, "fsdp", axis=1, tiled=True)
    replicas = lax.axis_size("rep")

    def add_rows(block_rows):
        return jnp.dot(features_all, block_rows, preferred_element_type=jnp.float32)

    one, two = derivatives(add_rows(lax.all_gather(gate_weight, "rep", axis=0, tiled=True)))
    weighted = cotangent.astype(jnp.float32) * up_act.astype(jnp.float32)
    coeff = (weighted * one).astype(jnp.bfloat16)
    bend = weighted * two
    rep_grad = lax.dot_general(
        features_all, coeff, (((0,), (0,)), ((), ())), preferred_element_type=jnp.float32
    ).astype(jnp.bfloat16)
    own_proj = jnp.dot(features_all, rep_grad, preferred_element_type=jnp.float32)
    grad_shard = lax.psum_scatter(rep_grad, "rep", scatter_dimension=0, tiled=True)
    mean_proj = add_rows(lax.all_gather(grad_shard, "rep", axis=0, tiled=True)) / replicas
    dev = own_proj - mean_proj
    curv_part = jnp.sum(bend * mean_proj * mean_proj, axis=0)
    spread_part = jnp.sum(bend * dev * dev, axis=0)
    curvature, spread = lax.psum((curv_part, spread_part), "rep")
    return grad_shard, curvature, spread / (replicas - 1)


def solution(mesh):
    zs, nr = mesh.shape["fsdp"], mesh.shape["rep"]
    body = functools.partial(units_split, zs, nr) if nr == 8 and zs <= 4 else tokens_split
    placed = (P("rep", "fsdp"),) * 4
    return jax.shard_map(
        body,
        mesh=mesh,
        in_specs=placed,
        out_specs=(P("rep", "fsdp"), P("fsdp"), P("fsdp")),
        check_vma=False,
    )
```

time: 456 us -> 349 us (0.77)
  waiting for transfers between devices: 351 us -> 0 us
  Pallas kernels: 0 us -> 220 us
  local copies, waits for them, and re-layouts: 3.83 us -> 36.1 us
  blocking collectives: 23.5 us -> 0 us
  matrix products: 62.4 us -> 83.2 us
  between operations: 13.8 us -> 0.7 us
  other arithmetic: 0.6 us -> 7.81 us
    all_gather x3 -> x0, waiting for transfers between devices: 247 us -> none  [the longest x1 84.3 us: shards(): features_all = lax.all_gather(tokens, 'fsdp', axis=1, tiled=True)]
    pallas_call x0 -> x2, Pallas kernels: none -> 220 us  [the longest x1 193 us: gather_all(): pl.pallas_call(functools.partial(gather_kernel, zs, nr), out_shape=(jax.S...]
    reduce_scatter x1 -> x0, waiting for transfers between devices: 102 us -> none  [shards(): lax.psum_scatter(rep_grad.astype(jnp.float32).astype(jnp.bfloat16), 'rep'...]
    psum x1 -> x0, blocking collectives: 23.5 us -> none  [shards(): curvature, spread_total = lax.psum((curv_part, spread_part), 'rep')]
    dot_general x4, matrix products: 62.4 us -> 83.2 us  [the longest x1 22.5 us: units_split(): lax.dot_general(t_rep, coeff, (((1,), (1,)), ((0,), (0,))), preferred_ele...]
    reshape x0 -> x3, local copies, waits for them, and re-layouts: none -> 10.8 us  [the longest x2 6.39 us: by_unit(): return a.reshape(a.shape[0], nr, cols).transpose(1, 0, 2)]
    unnamed x13 -> x6, local copies, waits for them, and re-layouts: 3.83 us -> 11.9 us
    convert_element_type x0 -> x2, other arithmetic: none -> 7.2 us  [the longest x1 3.96 us: units_split(): weighted = u_all.reshape(nr * rows, cols).astype(jnp.float32)]
  transfers between devices with their start and end apart: 4 -> 0, of which waited for: 4 -> 0; matrix products, arithmetic and copies ran while one was open for 1% -> 0% of each run, Pallas kernels for 0% -> 0%
where the time goes in v1:
time: 349 us; the launch traced here: 348 us
  Pallas kernels  220 us (63%)
  matrix products  83.2 us (24%)
  local copies, waits for them, and re-layouts  36.1 us (10%)
  other arithmetic  7.81 us (2%)
    pallas_call x1, Pallas kernels, gather_all(): pl.pallas_call(functools.partial(gather_kernel, zs, nr), out_shape=(jax.S...  193 us
    pallas_call x1, Pallas kernels, give_back(): pl.pallas_call(functools.partial(return_kernel, nr), out_shape=(jax.Shape...  27.2 us
    dot_general x1, matrix products, units_split(): lax.dot_general(t_rep, coeff, (((1,), (1,)), ((0,), (0,))), preferred_ele...  22.5 us
    dot_general x1, matrix products, units_split(): lax.dot_general(t_rep, rep_grad, (((2,), (1,)), ((0,), (0,))), preferred_...  20.5 us
    dot_general x1, matrix products, units_split(): jnp.dot(t_all, w_all.reshape(model, cols), preferred_element_type=jnp.flo...  20.2 us
    dot_general x1, matrix products, units_split(): mean = jnp.dot(t_all, grad_sum, preferred_element_type=jnp.float32) / nr  20 us
    unnamed x6, local copies, waits for them, and re-layouts  11.9 us

profile of v1, /device:TPU:0, one launch (start us, length us, event | category | flops | bytes accessed | tf_op | source)
XLA Modules:
  0.0 348.2 jit_solution(13720459904050243216)
XLA Ops:
  0.6 2.8 copy.22
  3.5 2.6 copy.23
  6.0 2.8 copy.25
  8.8 3.8 %copy.24 = bf16[512,1792]{0,1:T(8,128)(2,1)} copy(bf16[512,1792]{1,0:T(8,128)(2,1)} %param.7) | data formatting | bytes 3670016 | tf_op args[3]
  12.7 3.2 multiply_convert_fusion
  15.9 3.8 %copy.26 = bf16[512,8,224]{2,0,1:T(8,128)(2,1)} copy(bf16[512,8,224]{0,2,1:T(8,128)(2,1)} %bitcast.37) | data formatting | bytes 3670016 | tf_op jit(solution)/shard_map/reshape | solution.py:287
  19.7 193.3 %shard_map.67 = (bf16[4096,4096]{1,0:T(8,128)(2,1)}, bf16[8,512,224]{2,1,0:T(8,128)(2,1)}, bf16[8,512,224]{2,1,0:T(8,128)(2,1)}) custom-call(bf16[512,1024]{1,0:T(8,128)(2,1)} %t_ref.1, bf16[8,512,224]{2,1,0:T(8,128)(2,1)} %bitcast.32, bf16[8,512,224]{2,1,0:T(8,128)(2,1)} %bitcast.33), custom_call_target="tpu_custom_call" | custom-call | tf_op jit(solution)/shard_map/pallas_call | solution.py:211
  213.0 4.0 %bitcast_convert_fusion = f32[4096,224]{1,0:T(8,128)} fusion(bf16[8,512,224]{2,1,0:T(8,128)(2,1)} %get-tuple-element.9), kind=kLoop, calls=%fused_computation.16 | loop fusion | flops 917504 | bytes 5505024 | tf_op jit(solution)/shard_map/convert_element_type | solution.py:296
  217.0 0.0 copy-start
  217.0 5.6 %copy.27 = f32[4096,224]{0,1:T(8,128)} copy(f32[4096,224]{1,0:T(8,128)} %bitcast_convert_fusion) | data formatting | bytes 7340032 | tf_op jit(solution)/shard_map/convert_element_type | solution.py:296
  222.6 0.0 copy-done
  222.6 20.2 %fusion.3 = (bf16[4096,224]{0,1:T(8,128)(2,1)}, f32[4096,224]{0,1:T(8,128)}) fusion(f32[4096,224]{0,1:T(8,128)} %copy.27, bf16[4096,4096]{1,0:T(8,128)(2,1)} %get-tuple-element.8, bf16[4096,224]{1,0:T(8,128)(2,1)S(1)} %bitcast.43), kind=kOutput, calls=%fused_computation.9 | convolution fusion | flops 7524450304 | bytes 44564480 | tf_op jit(solution)/shard_map/dot_general | solution.py:294
  242.8 22.5 %fusion.10 = (bf16[4096,224]{0,1:T(8,128)(2,1)S(1)}, bf16[8,4096,224]{1,2,0:T(8,128)(2,1)}) fusion(bf16[8,512,4096]{2,1,0:T(8,128)(2,1)} %bitcast.30, bf16[28,8,8,512]{3,2,1,0:T(8,128)(2,1)} %bitcast.40), kind=kOutput, calls=%fused_computation.26 | convolution fusion | flops 7529955328 | bytes 51904512 | tf_op jit(solution)/shard_map/dot_general | solution.py:300
  265.3 20.5 %convolution_bitcast_fusion = f32[8,28,8,512]{3,2,1,0:T(8,128)} fusion(bf16[8,512,4096]{2,1,0:T(8,128)(2,1)} %bitcast.31, bf16[8,4096,224]{1,2,0:T(8,128)(2,1)} %get-tuple-element.26), kind=kOutput, calls=%fused_computation.17 | convolution fusion | flops 7516192768 | bytes 51904512 | tf_op jit(solution)/shard_map/dot_general | solution.py:303
  285.8 4.4 %copy.35 = f32[8,28,8,512]{3,2,0,1:T(8,128)} copy(f32[8,28,8,512]{3,2,1,0:T(8,128)} %convolution_bitcast_fusion) | data formatting | bytes 7340032 | tf_op jit(solution)/shard_map/reshape | solution.py:305
  290.2 20.0 %fusion.6 = (f32[224]{0:T(256)S(1)}, f32[224]{0:T(256)S(1)}) fusion(f32[4096,224]{0,1:T(8,128)} %copy.27, f32[4096,224]{0,1:T(8,128)} %get-tuple-element.24, f32[4096,224]{0,1:T(8,128)} %bitcast.38, bf16[4096,4096]{1,0:T(8,128)(2,1)} %get-tuple-element.8, bf16[4096,224]{0,1:T(8,128)(2,1)S(1)} %get-tuple-element.25), kind=kOutput, calls=%fused_computation.12 | convolution fusion | flops 7533625344 | bytes 46401280 | tf_op jit(solution)/shard_map/dot_general | solution.py:307
  310.2 0.6 select_maximum_fusion.p_ref
  310.8 2.5 copy.29
  313.3 27.2 %shard_map.68 = (bf16[8,512,224]{2,1,0:T(8,128)(2,1)}, f32[8,8,256]{2,1,0:T(8,128)}) custom-call(bf16[8,512,224]{2,1,0:T(8,128)(2,1)} %bitcast.34, f32[8,256]{1,0:T(8,128)} %select_maximum_fusion.p_ref), custom_call_target="tpu_custom_call" | custom-call | tf_op jit(solution)/shard_map/pallas_call | solution.py:257
  340.5 3.0 copy.32
  343.5 2.4 copy.33
  345.9 1.0 slice_reduce_fusion
  346.9 0.7 reshape_squeeze.7
  347.5 0.7 reshape_squeeze.6
  (1 shorter events, 0.0 us)
Async XLA Ops:
  217.0 5.6 %copy-start = (bf16[8,512,224]{2,1,0:T(8,128)(2,1)S(1)}, bf16[8,512,224]{2,1,0:T(8,128)(2,1)}, u32[]{:S(2)}) copy-start(bf16[8,512,224]{2,1,0:T(8,128)(2,1)} %get-tuple-element.10) | copy-start | bytes 5505028

commit v2 on v1

--- a/solution.py
+++ b/solution.py
@@ -36,6 +36,11 @@
     if b is True:
         return a
     return jnp.logical_and(a, b)
+
+
+def span(ref, k):
+    size = ref.shape[1] // 8
+    return ref.at[:, pl.ds(pl.multiple_of(k * size, size), size)]
 
 
 def greet(zs, r, z, masks, reach):
@@ -129,7 +134,7 @@
     for a, (src, dst) in enumerate(((w_ref, wa), (u_ref, ua))):
         for m in range(1, nr):
             copy = pltpu.make_async_remote_copy(
-                src_ref=src.at[flip(r, m)], dst_ref=dst.at[r],
+                src_ref=src.at[flip(r, m)], dst_ref=span(dst, r),
                 send_sem=s_a.at[a, m], recv_sem=r_a.at[a, m],
                 device_id=(flip(r, m), z), device_id_type=MESH,
             )
@@ -138,8 +143,6 @@
         copy.start()
     for q in (2, 3):
         go_xy(True, q, z)
-    for copy in swaps[nr - 1 :]:
-        copy.start()
     for q in range(4):
         go_core(True, 0, q, z)
     for copy in (keep, keep_w, keep_u):
@@ -148,8 +151,8 @@
         pl.ds(pl.multiple_of(r * rows, rows), rows), pl.ds(pl.multiple_of(z * feats, feats), feats)
     ]
     keep = pltpu.make_async_copy(tv, mine, s_l.at[0])
-    keep_w = pltpu.make_async_copy(wv, wa.at[r], s_l.at[1])
-    keep_u = pltpu.make_async_copy(uv, ua.at[r], s_l.at[2])
+    keep_w = pltpu.make_async_copy(wv, span(wa, r), s_l.at[1])
+    keep_u = pltpu.make_async_copy(uv, span(ua, r), s_l.at[2])
     for copy in (keep, keep_w, keep_u):
         copy.start()
 
@@ -162,7 +165,12 @@
             for q in range(4):
                 items.append((hops[m] + abs(d), m if d == 0 or q >= 2 else m, q, d))
     items.sort(key=lambda i: (i[0], abs(i[3])))
-    for _, m, q, d in items:
+    late = swaps[nr - 1 :]
+    for turn, m, q, d in items:
+        if turn > 2 and late:
+            for copy in late:
+                copy.start()
+            late = []
         zo = z if d == 0 else z + d
         valid = True if d == 0 else (zo >= 0 if d < 0 else zo < zs)
         got = pltpu.make_async_copy(region(ta, m, q, zo), region(ta, m, q, zo), r_t.at[rsem(m, q, zo)])
@@ -212,8 +220,8 @@
         functools.partial(gather_kernel, zs, nr),
         out_shape=(
             jax.ShapeDtypeStruct((rows * nr, feats * zs), tokens.dtype),
-            jax.ShapeDtypeStruct(w.shape, w.dtype),
-            jax.ShapeDtypeStruct(u.shape, u.dtype),
+            jax.ShapeDtypeStruct((w.shape[1], nr * w.shape[2]), w.dtype),
+            jax.ShapeDtypeStruct((u.shape[1], nr * u.shape[2]), u.dtype),
         ),
         in_specs=[ANY] * 3,
         out_specs=(ANY,) * 3,
@@ -234,14 +242,14 @@
     swaps = []
     for m in range(1, nr):
         there = flip(r, m)
-        for a, (src, dst) in enumerate(((g_ref.at[there], ga.at[r]), (p_ref, pa.at[r]))):
+        for a, (src, dst) in enumerate(((span(g_ref, there), ga.at[r]), (p_ref, pa.at[r]))):
             copy = pltpu.make_async_remote_copy(
                 src_ref=src, dst_ref=dst, send_sem=s_a.at[a, m], recv_sem=r_a.at[a, m],
                 device_id=(there, z), device_id_type=MESH,
             )
             copy.start()
             swaps.append(copy)
-    for src, mid, dst, a in ((g_ref.at[r], gv, ga.at[r], 0), (p_ref, pv, pa.at[r], 1)):
+    for src, mid, dst, a in ((span(g_ref, r), gv, ga.at[r], 0), (p_ref, pv, pa.at[r], 1)):
         copy = pltpu.make_async_copy(src, mid, s_l.at[a])
         copy.start()
         copy.wait()
@@ -257,13 +265,13 @@
     return pl.pallas_call(
         functools.partial(return_kernel, nr),
         out_shape=(
-            jax.ShapeDtypeStruct(grads.shape, grads.dtype),
+            jax.ShapeDtypeStruct((nr, grads.shape[0], grads.shape[1] // nr), grads.dtype),
             jax.ShapeDtypeStruct((nr,) + parts.shape, parts.dtype),
         ),
         in_specs=[ANY] * 2,
         out_specs=(ANY,) * 2,
         scratch_shapes=[
-            pltpu.VMEM(grads.shape[1:], grads.dtype),
+            pltpu.VMEM((grads.shape[0], grads.shape[1] // nr), grads.dtype),
             pltpu.VMEM(parts.shape, parts.dtype),
             dma((2, nr)), dma((2, nr)), dma((2,)),
         ],
@@ -284,33 +292,41 @@
     cols = hidden // nr
 
     def by_unit(a):
-        return a.reshape(a.shape[0], nr, cols).transpose(1, 0, 2)
+        return a.T.reshape(nr, cols, a.shape[0])
 
     product = cotangent.astype(jnp.float32) * up_act.astype(jnp.float32)
     t_all, w_all, u_all = gather_all(
         zs, nr, tokens, by_unit(gate_weight), by_unit(product.astype(jnp.bfloat16))
     )
     model = t_all.shape[1]
-    gate_pre = jnp.dot(t_all, w_all.reshape(model, cols), preferred_element_type=jnp.float32)
-    one, two = derivatives(gate_pre)
-    weighted = u_all.reshape(nr * rows, cols).astype(jnp.float32)
-    coeff = (weighted * one).astype(jnp.bfloat16).reshape(nr, rows, cols)
+
+    def project(left, block):
+        return lax.dot_general(left, block, (((1,), (1,)), ((), ())), preferred_element_type=jnp.float32)
+
+    one, two = derivatives(project(w_all, t_all))
+    weighted = u_all.astype(jnp.float32)
+    coeff = (weighted * one).astype(jnp.bfloat16)
     bend = weighted * two
-    t_rep = t_all.reshape(nr, rows, model)
-    rep_grad = lax.dot_general(
-        t_rep, coeff, (((1,), (1,)), ((0,), (0,))), preferred_element_type=jnp.float32
-    ).astype(jnp.bfloat16)
-    own = lax.dot_general(
-        t_rep, rep_grad, (((2,), (1,)), ((0,), (0,))), preferred_element_type=jnp.float32
-    ).reshape(nr * rows, cols)
-    grad_sum = jnp.sum(rep_grad.astype(jnp.float32), axis=0).astype(jnp.bfloat16)
-    mean = jnp.dot(t_all, grad_sum, preferred_element_type=jnp.float32) / nr
-    dev = own - mean
-    curv = jnp.sum(bend * mean * mean, axis=0)
-    spread = jnp.sum(bend * dev * dev, axis=0) / (nr - 1)
+    grad_acc, rep_grads = 0.0, []
+    for k in range(nr):
+        block = t_all[k * rows : (k + 1) * rows]
+        rep_grad = jnp.dot(
+            coeff[:, k * rows : (k + 1) * rows], block, preferred_element_type=jnp.float32
+        ).astype(jnp.bfloat16)
+        rep_grads.append(rep_grad)
+        grad_acc = grad_acc + rep_grad.astype(jnp.float32)
+    grad_sum = grad_acc.astype(jnp.bfloat16)
+    mean = project(grad_sum, t_all) / nr
+    curv = jnp.sum(bend * mean * mean, axis=1)
+    spread = 0.0
+    for k in range(nr):
+        part = slice(k * rows, (k + 1) * rows)
+        dev = project(rep_grads[k], t_all[part]) - mean[:, part]
+        spread = spread + jnp.sum(bend[:, part] * dev * dev, axis=1)
+    spread = spread / (nr - 1)
     parts = jnp.pad(jnp.stack([curv, spread]), ((0, 6), (0, -cols % 128)))
-    g_all, p_all = give_back(nr, grad_sum.reshape(nr, model // nr, cols), parts)
-    grad_rows = g_all.transpose(1, 0, 2).reshape(model // nr, hidden)
+    g_all, p_all = give_back(nr, grad_sum, parts)
+    grad_rows = g_all.reshape(hidden, model // nr).T
     stats = p_all[:, :, :cols]
     return grad_rows, stats[:, 0].reshape(hidden), stats[:, 1].reshape(hidden)
 

time: 349 us -> 338 us (0.968)
  local copies, waits for them, and re-layouts: 36.1 us -> 13.5 us
  matrix products: 83.2 us -> 105 us
  Pallas kernels: 220 us -> 215 us
  other arithmetic: 7.81 us -> 3.1 us
    dot_general x4 -> x18, matrix products: 83.2 us -> 105 us  [the longest x10 70.7 us: project(): lax.dot_general(left, block, (((1,), (1,)), ((), ())), preferred_element_...]
    unnamed x6 -> x36, local copies, waits for them, and re-layouts: 11.9 us -> 1.15 us
    convert_element_type x2 -> x0, other arithmetic: 7.2 us -> none  [the longest x1 3.96 us: units_split(): weighted = u_all.reshape(nr * rows, cols).astype(jnp.float32)]
    reshape x3 -> x1, local copies, waits for them, and re-layouts: 10.8 us -> 3.8 us  [units_split(): grad_rows = g_all.reshape(hidden, model // nr).T]
    convert_element_type x1 -> x0, local copies, waits for them, and re-layouts: 5.61 us -> none  [units_split(): weighted = u_all.reshape(nr * rows, cols).astype(jnp.float32)]
where the time goes in v2:
time: 338 us; the launch traced here: 337 us
  Pallas kernels  215 us (64%)
  matrix products  105 us (31%)
  local copies, waits for them, and re-layouts  13.5 us (4%)
    pallas_call x1, Pallas kernels, gather_all(): pl.pallas_call(functools.partial(gather_kernel, zs, nr), out_shape=(jax.S...  190 us
    dot_general x10, matrix products, project(): lax.dot_general(left, block, (((1,), (1,)), ((), ())), preferred_element_...  70.7 us
    dot_general x8, matrix products, units_split(): jnp.dot(coeff[:, k * rows:(k + 1) * rows], block, preferred_element_type=...  34.3 us
    pallas_call x1, Pallas kernels, give_back(): pl.pallas_call(functools.partial(return_kernel, nr), out_shape=(jax.Shape...  24.4 us

profile of v2, /device:TPU:0, one launch (start us, length us, event | category | flops | bytes accessed | tf_op | source)
XLA Modules:
  0.0 337.4 jit_solution(4481451024023128389)
XLA Ops:
  0.6 3.8 %copy.7 = bf16[1792,512]{1,0:T(8,128)(2,1)} copy(bf16[1792,512]{0,1:T(8,128)(2,1)} %bitcast.23) | data formatting | bytes 3670016 | tf_op jit(solution)/shard_map/transpose | solution.py:295
  4.5 2.5 fusion.29
  6.9 2.4 copy.8
  9.3 190.5 %shard_map.67 = (bf16[4096,4096]{1,0:T(8,128)(2,1)}, bf16[224,4096]{1,0:T(8,128)(2,1)}, bf16[224,4096]{1,0:T(8,128)(2,1)}) custom-call(bf16[512,1024]{1,0:T(8,128)(2,1)} %t_ref.1, bf16[8,224,512]{2,1,0:T(8,128)(2,1)} %bitcast.21, bf16[8,224,512]{2,1,0:T(8,128)(2,1)} %bitcast.22), custom_call_target="tpu_custom_call" | custom-call | tf_op jit(solution)/shard_map/pallas_call | solution.py:219
  199.8 18.4 %fusion.24 = (bf16[224,4096]{1,0:T(8,128)(2,1)S(1)}, f32[224,4096]{1,0:T(8,128)}) fusion(bf16[224,4096]{1,0:T(8,128)(2,1)} %get-tuple-element.8, bf16[224,4096]{1,0:T(8,128)(2,1)} %get-tuple-element.9, bf16[4096,4096]{1,0:T(8,128)(2,1)} %get-tuple-element.10), kind=kOutput, calls=%fused_computation.38 | convolution fusion | flops 7525367808 | bytes 42729472 | tf_op jit(solution)/shard_map/dot_general | solution.py:304
  218.2 0.0 copy-start.15
  218.2 4.0 %convolution_convert_fusion.1 = bf16[224,4096]{1,0:T(8,128)(2,1)S(1)} fusion(bf16[4096,4096]{1,0:T(8,128)(2,1)} %get-tuple-element.10, bf16[224,4096]{1,0:T(8,128)(2,1)S(1)} %get-tuple-element.17), kind=kOutput, calls=%fused_computation.5 | convolution fusion | flops 940441600 | bytes 6258688 | tf_op jit(solution)/shard_map/dot_general | solution.py:313
  222.2 0.0 copy-start.14
  222.2 4.0 %convolution_convert_fusion.2 = bf16[224,4096]{1,0:T(8,128)(2,1)S(1)} fusion(bf16[4096,4096]{1,0:T(8,128)(2,1)} %get-tuple-element.10, bf16[224,4096]{1,0:T(8,128)(2,1)S(1)} %get-tuple-element.17), kind=kOutput, calls=%fused_computation.6 | convolution fusion | flops 940441600 | bytes 6258688 | tf_op jit(solution)/shard_map/dot_general | solution.py:313
  226.2 0.0 copy-start.12
  226.2 4.0 %convolution_convert_fusion.3 = bf16[224,4096]{1,0:T(8,128)(2,1)S(1)} fusion(bf16[4096,4096]{1,0:T(8,128)(2,1)} %get-tuple-element.10, bf16[224,4096]{1,0:T(8,128)(2,1)S(1)} %get-tuple-element.17), kind=kOutput, calls=%fused_computation.7 | convolution fusion | flops 940441600 | bytes 6258688 | tf_op jit(solution)/shard_map/dot_general | solution.py:313
  230.2 0.0 copy-start.10
  230.2 4.0 %convolution_convert_fusion.4 = bf16[224,4096]{1,0:T(8,128)(2,1)S(1)} fusion(bf16[4096,4096]{1,0:T(8,128)(2,1)} %get-tuple-element.10, bf16[224,4096]{1,0:T(8,128)(2,1)S(1)} %get-tuple-element.17), kind=kOutput, calls=%fused_computation.8 | convolution fusion | flops 940441600 | bytes 6258688 | tf_op jit(solution)/shard_map/dot_general | solution.py:313
  234.2 0.0 copy-start.8
  234.2 4.0 %convolution_convert_fusion.5 = bf16[224,4096]{1,0:T(8,128)(2,1)S(1)} fusion(bf16[4096,4096]{1,0:T(8,128)(2,1)} %get-tuple-element.10, bf16[224,4096]{1,0:T(8,128)(2,1)S(1)} %get-tuple-element.17), kind=kOutput, calls=%fused_computation.9 | convolution fusion | flops 940441600 | bytes 6258688 | tf_op jit(solution)/shard_map/dot_general | solution.py:313
  238.2 0.0 copy-start.6
  238.2 4.0 %convolution_convert_fusion.6 = bf16[224,4096]{1,0:T(8,128)(2,1)S(1)} fusion(bf16[4096,4096]{1,0:T(8,128)(2,1)} %get-tuple-element.10, bf16[224,4096]{1,0:T(8,128)(2,1)S(1)} %get-tuple-element.17), kind=kOutput, calls=%fused_computation.10 | convolution fusion | flops 940441600 | bytes 6258688 | tf_op jit(solution)/shard_map/dot_general | solution.py:313
  242.1 0.0 copy-done.15
  242.2 0.0 copy-start.4
  242.2 4.0 %convolution_convert_fusion.7 = bf16[224,4096]{1,0:T(8,128)(2,1)S(1)} fusion(bf16[4096,4096]{1,0:T(8,128)(2,1)} %get-tuple-element.10, bf16[224,4096]{1,0:T(8,128)(2,1)S(1)} %get-tuple-element.17), kind=kOutput, calls=%fused_computation.11 | convolution fusion | flops 940441600 | bytes 6258688 | tf_op jit(solution)/shard_map/dot_general | solution.py:313
  246.1 0.0 copy-done.14
  246.2 0.0 copy-done.12
  246.2 0.0 copy-done.10
  246.2 0.0 copy-done.8
  246.2 0.0 copy-done.6
  246.2 0.0 copy-done.4
  246.2 0.0 copy-start.2
  246.2 6.5 %add_convert_fusion = (bf16[224,4096]{1,0:T(8,128)(2,1)S(1)}, bf16[224,4096]{1,0:T(8,128)(2,1)}) fusion(bf16[224,4096]{1,0:T(8,128)(2,1)S(1)} %convolution_convert_fusion.1, bf16[224,4096]{1,0:T(8,128)(2,1)S(1)} %convolution_convert_fusion.2, bf16[224,4096]{1,0:T(8,128)(2,1)S(1)} %convolution_convert_fusion.3, ...), kind=kOutput, calls=%fused_computation.43 | convolution fusion | flops 955121664 | bytes 20938752 | tf_op jit(solution)/shard_map/dot_general | solution.py:313
  252.7 0.0 copy-done.2
  252.7 0.0 copy-start
  252.7 20.9 %fusion.28 = (f32[224]{0:T(256)S(1)}, f32[224,4096]{1,0:T(8,128)}, f32[224,4096]{1,0:T(8,128)}) fusion(f32[224,4096]{1,0:T(8,128)} %get-tuple-element.18, bf16[224,4096]{1,0:T(8,128)(2,1)} %get-tuple-element.8, bf16[224,4096]{1,0:T(8,128)(2,1)S(1)} %get-tuple-element.19.g_ref, bf16[4096,4096]{1,0:T(8,128)(2,1)} %get-tuple-element.10), kind=kOutput, calls=%fused_computation.42 | convolution fusion | flops 7530872832 | bytes 48235392 | tf_op jit(solution)/shard_map/dot_general | solution.py:304
  273.7 0.0 copy-done
  273.7 0.0 copy-start.13
  273.7 0.0 copy-start.16
  273.7 0.0 copy-start.17
  273.7 4.6 %fusion.61 = f32[224]{0:T(256)S(1)} fusion(bf16[224,4096]{1,0:T(8,128)(2,1)} %copy-done.14, bf16[4096,4096]{1,0:T(8,128)(2,1)} %get-tuple-element.10, f32[224,4096]{1,0:T(8,128)} %get-tuple-element.21, f32[224,4096]{1,0:T(8,128)} %get-tuple-element.16), kind=kOutput, calls=%fused_computation.58 | convolution fusion | flops 939982592 | bytes 6947712 | tf_op jit(solution)/shard_map/dot_general | solution.py:304
  278.3 0.0 copy-done.13
  278.3 0.0 copy-done.16
  278.3 1.1 copy-done.17
  279.4 0.0 copy-start.11
  279.4 3.8 %fusion.66 = f32[224]{0:T(256)S(1)} fusion(bf16[224,4096]{1,0:T(8,128)(2,1)S(1)} %copy-done.13, bf16[4096,4096]{1,0:T(8,128)(2,1)} %get-tuple-element.10, f32[224,4096]{1,0:T(8,128)S(1)} %copy-done.17, f32[224,4096]{1,0:T(8,128)S(1)} %copy-done.16), kind=kOutput, calls=%fused_computation.60 | convolution fusion | flops 939982592 | bytes 6947712 | tf_op jit(solution)/shard_map/dot_general | solution.py:304
  283.2 0.0 copy-done.11
  283.3 0.0 copy-start.9
  283.3 3.9 %fusion.71 = f32[224]{0:T(256)S(1)} fusion(bf16[224,4096]{1,0:T(8,128)(2,1)S(1)} %copy-done.11, bf16[4096,4096]{1,0:T(8,128)(2,1)} %get-tuple-element.10, f32[224,4096]{1,0:T(8,128)S(1)} %copy-done.17, f32[224,4096]{1,0:T(8,128)S(1)} %copy-done.16), kind=kOutput, calls=%fused_computation.62 | convolution fusion | flops 939982592 | bytes 6947712 | tf_op jit(solution)/shard_map/dot_general | solution.py:304
  287.1 0.0 copy-done.9
  287.1 0.0 copy-start.7
  287.1 3.8 %fusion.76 = f32[224]{0:T(256)S(1)} fusion(bf16[224,4096]{1,0:T(8,128)(2,1)S(1)} %copy-done.9, bf16[4096,4096]{1,0:T(8,128)(2,1)} %get-tuple-element.10, f32[224,4096]{1,0:T(8,128)S(1)} %copy-done.17, f32[224,4096]{1,0:T(8,128)S(1)} %copy-done.16), kind=kOutput, calls=%fused_computation.64 | convolution fusion | flops 939982592 | bytes 6947712 | tf_op jit(solution)/shard_map/dot_general | solution.py:304
  291.0 0.0 copy-done.7
  291.0 0.0 copy-start.5
  291.0 3.9 %fusion.81 = f32[224]{0:T(256)S(1)} fusion(bf16[224,4096]{1,0:T(8,128)(2,1)S(1)} %copy-done.7, bf16[4096,4096]{1,0:T(8,128)(2,1)} %get-tuple-element.10, f32[224,4096]{1,0:T(8,128)S(1)} %copy-done.17, f32[224,4096]{1,0:T(8,128)S(1)} %copy-done.16), kind=kOutput, calls=%fused_computation.66 | convolution fusion | flops 939982592 | bytes 6947712 | tf_op jit(solution)/shard_map/dot_general | solution.py:304
  294.8 0.0 copy-done.5
  294.9 0.0 copy-start.3
  294.9 3.8 %fusion.86 = f32[224]{0:T(256)S(1)} fusion(bf16[224,4096]{1,0:T(8,128)(2,1)S(1)} %copy-done.5, bf16[4096,4096]{1,0:T(8,128)(2,1)} %get-tuple-element.10, f32[224,4096]{1,0:T(8,128)S(1)} %copy-done.17, f32[224,4096]{1,0:T(8,128)S(1)} %copy-done.16), kind=kOutput, calls=%fused_computation.68 | convolution fusion | flops 939982592 | bytes 6947712 | tf_op jit(solution)/shard_map/dot_general | solution.py:304
  298.7 0.0 copy-done.3
  298.7 0.0 copy-start.1
  298.7 3.8 %fusion.91 = f32[224]{0:T(256)S(1)} fusion(bf16[224,4096]{1,0:T(8,128)(2,1)S(1)} %copy-done.3, bf16[4096,4096]{1,0:T(8,128)(2,1)} %get-tuple-element.10, f32[224,4096]{1,0:T(8,128)S(1)} %copy-done.17, f32[224,4096]{1,0:T(8,128)S(1)} %copy-done.16), kind=kOutput, calls=%fused_computation.70 | convolution fusion | flops 939982592 | bytes 6947712 | tf_op jit(solution)/shard_map/dot_general | solution.py:304
  302.6 0.0 copy-done.1
  302.6 3.7 %fusion.56 = f32[224]{0:T(256)S(1)} fusion(bf16[224,4096]{1,0:T(8,128)(2,1)S(1)} %copy-done.1, bf16[4096,4096]{1,0:T(8,128)(2,1)} %get-tuple-element.10, f32[224,4096]{1,0:T(8,128)S(1)} %copy-done.17, f32[224,4096]{1,0:T(8,128)S(1)} %copy-done.16), kind=kOutput, calls=%fused_computation.56 | convolution fusion | flops 939982592 | bytes 6947712 | tf_op jit(solution)/shard_map/dot_general | solution.py:304
  306.3 0.6 select_maximum_fusion.p_ref
  306.9 24.4 %shard_map.68 = (bf16[8,224,512]{2,1,0:T(8,128)(2,1)}, f32[8,8,256]{2,1,0:T(8,128)}) custom-call(bf16[224,4096]{1,0:T(8,128)(2,1)} %copy-done, f32[8,256]{1,0:T(8,128)} %select_maximum_fusion.p_ref), custom_call_target="tpu_custom_call" | custom-call | tf_op jit(solution)/shard_map/pallas_call | solution.py:265
  331.3 3.8 %copy.9 = bf16[1792,512]{0,1:T(8,128)(2,1)} copy(bf16[1792,512]{1,0:T(8,128)(2,1)} %bitcast.25) | data formatting | bytes 3670016 | tf_op jit(solution)/shard_map/reshape | solution.py:329
  335.1 1.0 slice_reduce_fusion
  336.0 0.7 reshape_squeeze.7
  336.7 0.7 reshape_squeeze.6
  (1 shorter events, 0.0 us)
Async XLA Ops:
  218.2 23.9 %copy-start.15 = (bf16[224,4096]{1,0:T(8,128)(2,1)}, bf16[224,4096]{1,0:T(8,128)(2,1)S(1)}, u32[]{:S(2)}) copy-start(bf16[224,4096]{1,0:T(8,128)(2,1)S(1)} %get-tuple-element.17) | copy-start | bytes 5505028
  222.2 24.0 %copy-start.14 = (bf16[224,4096]{1,0:T(8,128)(2,1)}, bf16[224,4096]{1,0:T(8,128)(2,1)S(1)}, u32[]{:S(2)}) copy-start(bf16[224,4096]{1,0:T(8,128)(2,1)S(1)} %convolution_convert_fusion.1) | copy-start | bytes 5505028
  226.2 20.0 %copy-start.12 = (bf16[224,4096]{1,0:T(8,128)(2,1)}, bf16[224,4096]{1,0:T(8,128)(2,1)S(1)}, u32[]{:S(2)}) copy-start(bf16[224,4096]{1,0:T(8,128)(2,1)S(1)} %convolution_convert_fusion.2) | copy-start | bytes 5505028
  230.2 16.0 %copy-start.10 = (bf16[224,4096]{1,0:T(8,128)(2,1)}, bf16[224,4096]{1,0:T(8,128)(2,1)S(1)}, u32[]{:S(2)}) copy-start(bf16[224,4096]{1,0:T(8,128)(2,1)S(1)} %convolution_convert_fusion.3) | copy-start | bytes 5505028
  234.2 12.0 %copy-start.8 = (bf16[224,4096]{1,0:T(8,128)(2,1)}, bf16[224,4096]{1,0:T(8,128)(2,1)S(1)}, u32[]{:S(2)}) copy-start(bf16[224,4096]{1,0:T(8,128)(2,1)S(1)} %convolution_convert_fusion.4) | copy-start | bytes 5505028
  238.2 8.0 %copy-start.6 = (bf16[224,4096]{1,0:T(8,128)(2,1)}, bf16[224,4096]{1,0:T(8,128)(2,1)S(1)}, u32[]{:S(2)}) copy-start(bf16[224,4096]{1,0:T(8,128)(2,1)S(1)} %convolution_convert_fusion.5) | copy-start | bytes 5505028
  242.2 4.0 %copy-start.4 = (bf16[224,4096]{1,0:T(8,128)(2,1)}, bf16[224,4096]{1,0:T(8,128)(2,1)S(1)}, u32[]{:S(2)}) copy-start(bf16[224,4096]{1,0:T(8,128)(2,1)S(1)} %convolution_convert_fusion.6) | copy-start | bytes 5505028
  246.2 6.5 %copy-start.2 = (bf16[224,4096]{1,0:T(8,128)(2,1)}, bf16[224,4096]{1,0:T(8,128)(2,1)S(1)}, u32[]{:S(2)}) copy-start(bf16[224,4096]{1,0:T(8,128)(2,1)S(1)} %convolution_convert_fusion.7) | copy-start | bytes 5505028
  252.7 20.9 %copy-start = (bf16[224,4096]{1,0:T(8,128)(2,1)}, bf16[224,4096]{1,0:T(8,128)(2,1)S(1)}, u32[]{:S(2)}) copy-start(bf16[224,4096]{1,0:T(8,128)(2,1)S(1)} %get-tuple-element.19.g_ref) | copy-start | bytes 5505028
  273.7 4.6 %copy-start.13 = (bf16[224,4096]{1,0:T(8,128)(2,1)S(1)}, bf16[224,4096]{1,0:T(8,128)(2,1)}, u32[]{:S(2)}) copy-start(bf16[224,4096]{1,0:T(8,128)(2,1)} %copy-done.12) | copy-start | bytes 5505028
  273.7 4.7 %copy-start.16 = (f32[224,4096]{1,0:T(8,128)S(1)}, f32[224,4096]{1,0:T(8,128)}, u32[]{:S(2)}) copy-start(f32[224,4096]{1,0:T(8,128)} %get-tuple-element.16) | copy-start | bytes 11010052
  273.7 5.7 %copy-start.17 = (f32[224,4096]{1,0:T(8,128)S(1)}, f32[224,4096]{1,0:T(8,128)}, u32[]{:S(2)}) copy-start(f32[224,4096]{1,0:T(8,128)} %get-tuple-element.21) | copy-start | bytes 11010052
  279.4 3.8 %copy-start.11 = (bf16[224,4096]{1,0:T(8,128)(2,1)S(1)}, bf16[224,4096]{1,0:T(8,128)(2,1)}, u32[]{:S(2)}) copy-start(bf16[224,4096]{1,0:T(8,128)(2,1)} %copy-done.10) | copy-start | bytes 5505028
  283.3 3.9 %copy-start.9 = (bf16[224,4096]{1,0:T(8,128)(2,1)S(1)}, bf16[224,4096]{1,0:T(8,128)(2,1)}, u32[]{:S(2)}) copy-start(bf16[224,4096]{1,0:T(8,128)(2,1)} %copy-done.8) | copy-start | bytes 5505028
  287.1 3.9 %copy-start.7 = (bf16[224,4096]{1,0:T(8,128)(2,1)S(1)}, bf16[224,4096]{1,0:T(8,128)(2,1)}, u32[]{:S(2)}) copy-start(bf16[224,4096]{1,0:T(8,128)(2,1)} %copy-done.6) | copy-start | bytes 5505028
  291.0 3.9 %copy-start.5 = (bf16[224,4096]{1,0:T(8,128)(2,1)S(1)}, bf16[224,4096]{1,0:T(8,128)(2,1)}, u32[]{:S(2)}) copy-start(bf16[224,4096]{1,0:T(8,128)(2,1)} %copy-done.4) | copy-start | bytes 5505028
  294.9 3.9 %copy-start.3 = (bf16[224,4096]{1,0:T(8,128)(2,1)S(1)}, bf16[224,4096]{1,0:T(8,128)(2,1)}, u32[]{:S(2)}) copy-start(bf16[224,4096]{1,0:T(8,128)(2,1)} %copy-done.2) | copy-start | bytes 5505028
  298.7 3.9 %copy-start.1 = (bf16[224,4096]{1,0:T(8,128)(2,1)S(1)}, bf16[224,4096]{1,0:T(8,128)(2,1)}, u32[]{:S(2)}) copy-start(bf16[224,4096]{1,0:T(8,128)(2,1)} %get-tuple-element.20) | copy-start | bytes 5505028
